TPU v7x, 32 devices: a whole 2x2x4 slice. The times are simulated.
32 devices in a mesh: fsdp: 2 (over y), tensor: 4 (over x, core), replica: 4 (over z).
Axes of the slice: x: 2, y: 2, z: 4, core: 2. Of those that a mesh axis runs over, the one named last changes fastest.
Arguments:
- gradient: bfloat16 [4, 4096, 8192], P('replica', 'fsdp', 'tensor'), may hold values from -400 to 400, as said below
- momentum: float32 [4, 4096, 8192], P('replica', 'fsdp', 'tensor'), may hold values from -6 to 6
- basis: float32 [8192, 256], P('tensor', 'fsdp'), may hold values from -0.0625 to 0.0625
Outputs:
- update: bfloat16 [4096, 8192], P('fsdp', 'tensor')
- momentum_new: float32 [4, 4096, 8192], P('replica', 'fsdp', 'tensor')
- basis_new: float32 [8192, 256], P('tensor', 'fsdp')
Inputs may be any that keep to these rules, and one draw needn't show every extreme that they name: gradient entries are finite real numbers.
All inputs are finite; a program needn't handle non-finite values.
Results may differ from a plain program's by a relative error of at most 0.001.
Values sent between devices are 32-bit elements; how exact they have to be, the bound alone decides.
A program may use at most 128 MiB of HBM per device.

v0:
```python
import jax
import jax.numpy as jnp
from jax import lax
from jax.sharding import PartitionSpec as P

M_ROWS = 4096
NCOLS = 8192
RANK = 256
HIGH = lax.Precision.HIGHEST


def local(gradient, momentum, basis):
    replicas = lax.axis_size("replica")
    rank_local = basis.shape[1]
    buffer = momentum[0] + gradient[0].astype(jnp.float32)
    partial_value = jnp.dot(
        buffer,
        lax.all_gather(basis, "fsdp", axis=1, tiled=True),
        precision=HIGH,
        preferred_element_type=jnp.float32,
    )
    left = lax.psum(partial_value, ("tensor", "replica")) / replicas
    local_gram = jnp.dot(left.T, left, precision=HIGH, preferred_element_type=jnp.float32)
    gram = lax.psum(local_gram, "fsdp")
    chol = jnp.linalg.cholesky(gram)
    ortho = lax.linalg.triangular_solve(chol, left, left_side=False, lower=True, transpose_a=True)
    right_part = jnp.dot(buffer.T, ortho, precision=HIGH, preferred_element_type=jnp.float32)
    right = lax.psum(right_part, ("fsdp", "replica")) / replicas
    squares = lax.psum(jnp.sum(right * right, axis=0), "tensor")
    norms = jnp.sqrt(squares + 1e-12)
    basis_full = right / norms
    lowrank = jnp.dot(ortho, right.T, precision=HIGH, preferred_element_type=jnp.float32)
    momentum_new = (buffer - 0.05 * lowrank)[None]
    scale = (M_ROWS * NCOLS / RANK) ** 0.5
    update = (
        scale * jnp.dot(ortho, basis_full.T, precision=HIGH, preferred_element_type=jnp.float32)
    ).astype(jnp.bfloat16)
    offset = lax.axis_index("fsdp") * rank_local
    basis_new = lax.dynamic_slice_in_dim(basis_full, offset, rank_local, 1)
    return (update, momentum_new, basis_new)


def solution(mesh):
    return jax.shard_map(
        local,
        mesh=mesh,
        in_specs=(
            P("replica", "fsdp", "tensor"),
            P("replica", "fsdp", "tensor"),
            P("tensor", "fsdp"),
        ),
        out_specs=(P("fsdp", "tensor"), P("replica", "fsdp", "tensor"), P("tensor", "fsdp")),
        check_vma=False,
    )
```

profile of v0, /device:TPU:0, one launch (start us, length us, event | category | flops | bytes accessed | tf_op | source)
XLA Modules:
  0.0 472.0 jit_solution(12130268575645546304)
XLA Ops:
  7.2 0.0 all-gather.2.cloned.1.call-start
  7.2 0.7 all-gather.2.cloned.1.call-update
  7.9 0.0 all-reduce.5.cloned.1.call-start
  7.9 37.4 %all-gather.2.cloned.1.call-done = f32[2048,256]{1,0:T(8,128)} async-done(((f32[2048,128]{1,0:T(8,128)}), f32[2048,256]{1,0:T(8,128)}) %all-gather.2.cloned.1.call-update) | async-done | bytes 2097168 | tf_op jit(solution)/shard_map/all_gather | solution.py:18
  45.3 18.8 %fusion.2 = f32[2048,256]{1,0:T(8,128)} fusion(f32[2048,256]{1,0:T(8,128)} %all-gather.2.cloned.1.call-done, f32[1,2048,2048]{2,1,0:T(8,128)} %param.4, bf16[1,2048,2048]{2,1,0:T(8,128)(2,1)} %param.3), kind=kOutput, calls=%fused_computation.5 | convolution fusion | flops 12893290496 | bytes 29360128 | tf_op jit(solution)/shard_map/dot_general | solution.py:16
  64.2 0.0 all-reduce.5.cloned.1.call-update
  64.2 0.0 all-reduce.7.cloned.1.call-start
  64.3 98.4 %all-reduce.5.cloned.1.call-done = f32[2048,256]{1,0:T(8,128)} async-done(((f32[2048,256]{1,0:T(8,128)}), f32[2048,256]{1,0:T(8,128)}) %all-reduce.5.cloned.1.call-update) | async-done | bytes 2097168 | tf_op jit(solution)/shard_map/psum | solution.py:22
  162.6 6.4 %fusion.19 = f32[256,256]{0,1:T(8,128)} fusion(f32[2048,256]{1,0:T(8,128)} %all-reduce.5.cloned.1.call-done), kind=kOutput, calls=%fused_computation.47 | convolution fusion | flops 1611137024 | bytes 2359296 | tf_op jit(solution)/shard_map/dot_general | solution.py:23
  169.0 0.0 all-reduce.7.cloned.1.call-update
  169.1 0.6 all-reduce.9.cloned.1.call-start
  169.6 1.7 broadcast_multiply_fusion
  171.4 20.4 %all-reduce.7.cloned.1.call-done = f32[256,256]{0,1:T(8,128)} async-done(((f32[256,256]{0,1:T(8,128)}), f32[256,256]{0,1:T(8,128)}) %all-reduce.7.cloned.1.call-update) | async-done | bytes 262160 | tf_op jit(solution)/shard_map/psum | solution.py:24
  191.7 1.1 copy.7
  192.8 1.0 fusion.9
  193.8 11.7 %cholesky.50 = f32[128,128]{1,0:T(8,128)S(1)} custom-call(f32[128,128]{1,0:T(8,128)S(1)} %cholesky.118), custom_call_target="Cholesky" | custom-call | tf_op jit(solution)/shard_map/jit(cholesky)/cholesky | solution.py:25
  205.6 9.8 %custom-call.14 = f32[1,128,128]{1,2,0:T(8,128)S(1)} custom-call(f32[1,128,128]{2,1,0:T(8,128)S(1)} %get-tuple-element.24), custom_call_target="InvertDiagBlocksLowerTriangular" | custom-call | tf_op jit(solution)/shard_map/jit(cholesky)/cholesky | solution.py:25
  215.4 0.2 constant_dynamic-update-slice_fusion
  215.6 0.3 convolution_subtract_fusion.1
  215.9 11.7 %cholesky.105 = f32[128,128]{1,0:T(8,128)S(1)} custom-call(f32[128,128]{1,0:T(8,128)S(1)} %convolution_subtract_fusion.1), custom_call_target="Cholesky" | custom-call | tf_op jit(solution)/shard_map/jit(cholesky)/cholesky | solution.py:25
  227.6 0.6 compare_reduce_fusion
  229.6 0.1 triangular_solve.58
  229.7 4.2 while.1
  229.9 0.6 fusion.28
  230.5 1.4 bitcast_dynamic-update-slice_fusion.2
  231.9 0.6 fusion.28
  232.5 1.4 bitcast_dynamic-update-slice_fusion.2
  233.9 19.7 %custom-call.15 = f32[2,128,128]{1,2,0:T(8,128)S(1)} custom-call(f32[2,128,128]{2,1,0:T(8,128)S(1)} %get-tuple-element.10), custom_call_target="InvertDiagBlocksLowerTriangular" | custom-call | tf_op jit(solution)/shard_map/triangular_solve | solution.py:26
  253.5 1.1 fusion.6
  254.6 1.8 convolution_subtract_fusion
  256.5 1.1 fusion.10
  257.6 0.0 copy-start.1
  257.6 1.0 copy-done.1
  258.5 31.3 %fusion = f32[2048,256]{1,0:T(8,128)} fusion(f32[1,2048,2048]{2,1,0:T(8,128)} %param.4, bf16[1,2048,2048]{2,1,0:T(8,128)(2,1)} %param.3, f32[2048,128]{0,1:T(8,128)S(1)} %fusion.10, f32[2048,128]{0,1:T(8,128)S(1)} %fusion.6), kind=kOutput, calls=%fused_computation.3 | convolution fusion | flops 12893814784 | bytes 29360128 | tf_op jit(solution)/shard_map/dot_general | solution.py:27
  289.8 0.0 all-reduce.9.cloned.1.call-update
  289.8 102.4 %all-reduce.9.cloned.1.call-done = f32[2048,256]{1,0:T(8,128)} async-done(((f32[2048,256]{1,0:T(8,128)}), f32[2048,256]{1,0:T(8,128)}) %all-reduce.9.cloned.1.call-update) | async-done | bytes 2097168 | tf_op jit(solution)/shard_map/psum | solution.py:28
  392.3 0.0 copy-start
  392.3 2.0 multiply_reduce_fusion
  394.3 6.4 %psum.31 = f32[256]{0:T(256)S(1)} all-reduce(f32[256]{0:T(256)S(1)} %multiply_reduce_fusion), channel_id=1, replica_groups=mesh['fsdp'=2,'tensor'=4,'replica'=4] {'tensor'}, use_global_device_ids=true, to_apply=%region_8.9 | all-reduce | flops 256 | bytes 2048 | tf_op jit(solution)/shard_map/psum | solution.py:29
  400.7 0.0 copy-done
  400.7 0.0 copy-start.2
  400.7 0.1 multiply_divide_fusion
  400.9 1.1 copy-done.2
  401.9 28.8 %multiply_convert_fusion = bf16[2048,2048]{1,0:T(8,128)(2,1)} fusion(f32[2048,256]{1,0:T(8,128)S(1)} %multiply_divide_fusion, f32[2048,128]{0,1:T(8,128)S(1)} %copy-done.2, f32[2048,128]{0,1:T(8,128)S(1)} %fusion.6), kind=kOutput, calls=%fused_computation.8 | convolution fusion | flops 12893814784 | bytes 12582912 | tf_op jit(solution)/shard_map/dot_general | solution.py:36
  430.8 1.0 constant_dynamic-slice_fusion.1
  431.8 33.1 %fusion.4 = f32[1,2048,2048]{2,1,0:T(8,128)} fusion(f32[1,2048,2048]{2,1,0:T(8,128)} %param.4, bf16[1,2048,2048]{2,1,0:T(8,128)(2,1)} %param.3, f32[2048,256]{1,0:T(8,128)S(1)} %copy-done, f32[2048,128]{0,1:T(8,128)S(1)} %copy-done.2, f32[2048,128]{0,1:T(8,128)S(1)} %fusion.6), kind=kOutput, calls=%fused_computation.7 | convolution fusion | flops 12902727680 | bytes 46137344 | tf_op jit(solution)/shard_map/dot_general | solution.py:32
  (10 shorter events, 0.2 us)
Async XLA Ops:
  7.2 38.2 %all-gather.2.cloned.1.call-start = ((), (), s32[]{:S(2)}) async-start(), calls=%async_computation | async-start | bytes 3145728 | tf_op jit(solution)/shard_map/all_gather | solution.py:18
  7.9 154.7 %all-reduce.5.cloned.1.call-start = ((), (), s32[]{:S(2)}) async-start(), calls=%async_computation.1 | async-start | bytes 4194304 | tf_op jit(solution)/shard_map/psum | solution.py:22
  64.2 127.5 %all-reduce.7.cloned.1.call-start = ((), (), s32[]{:S(2)}) async-start(), calls=%async_computation.2 | async-start | bytes 524288 | tf_op jit(solution)/shard_map/psum | solution.py:24
  169.1 223.2 %all-reduce.9.cloned.1.call-start = ((), (), s32[]{:S(2)}) async-start(), calls=%async_computation.3 | async-start | bytes 4194304 | tf_op jit(solution)/shard_map/psum | solution.py:28
  257.6 1.0 copy-start.1
  392.3 8.4 %copy-start = (f32[2048,256]{1,0:T(8,128)S(1)}, f32[2048,256]{1,0:T(8,128)}, u32[]{:S(2)}) copy-start(f32[2048,256]{1,0:T(8,128)} %all-reduce.9.cloned.1.call-done) | copy-start | bytes 6291460
  400.7 1.2 copy-start.2
Sparse Core Ops, SparseCore 0:
  9.5 35.7 all-gather.1
  64.3 98.2 all-reduce.4
  169.2 22.4 all-reduce.6
  289.9 102.2 all-reduce.8
where the time goes:
time: 478 us; the launch traced here: 472 us
  waiting for transfers between devices  259 us (54%)
  matrix products  123 us (26%)
  other arithmetic  58.6 us (12%)
  between operations  15.7 us (3%)
  local copies, waits for them, and re-layouts  8.2 us (2%)
  blocking collectives  6.38 us (1%)
    psum x1, waiting for transfers between devices, local(): right = lax.psum(right_part, ('fsdp', 'replica')) / replicas  102 us
    psum x1, waiting for transfers between devices, local(): left = lax.psum(partial_value, ('tensor', 'replica')) / replicas  98.4 us
    all_gather x1, waiting for transfers between devices, local(): lax.all_gather(basis, 'fsdp', axis=1, tiled=True)  37.4 us
    another operation x6, other arithmetic, local(): chol = jnp.linalg.cholesky(gram)  34 us
    dot_general x1, matrix products, local(): jnp.dot(ortho, right.T, precision=HIGH, preferred_element_type=jnp.float32)  33.1 us
    dot_general x1, matrix products, local(): jnp.dot(buffer.T, ortho, precision=HIGH, preferred_element_type=jnp.float32)  31.3 us
    dot_general x1, matrix products, local(): jnp.dot(ortho, basis_full.T, precision=HIGH, preferred_element_type=jnp.f...  28.8 us
    psum x1, waiting for transfers between devices, local(): gram = lax.psum(local_gram, 'fsdp')  20.4 us
  transfers between devices with their start and end apart: 4, of which 4 were waited for; matrix products, arithmetic and copies ran while one was open for 0% of the time, Pallas kernels for 0%

commit v1 on v0

--- a/solution.py
+++ b/solution.py
@@ -19,7 +19,7 @@
         precision=HIGH,
         preferred_element_type=jnp.float32,
     )
-    left = lax.psum(partial_value, ("tensor", "replica")) / replicas
+    left = lax.psum(lax.psum(partial_value, "replica"), "tensor") / replicas
     local_gram = jnp.dot(left.T, left, precision=HIGH, preferred_element_type=jnp.float32)
     gram = lax.psum(local_gram, "fsdp")
     chol = jnp.linalg.cholesky(gram)

time: 478 us -> 520 us (1.088)
  waiting for transfers between devices: 259 us -> 301 us
    psum x1 -> x2, waiting for transfers between devices: 98.4 us -> 139 us  [local(): left = lax.psum(lax.psum(partial_value, 'replica'), 'tensor') / replicas]
  transfers between devices with their start and end apart: 4 -> 5, of which waited for: 4 -> 5; matrix products, arithmetic and copies ran while one was open for 0% -> 0% of each run, Pallas kernels for 0% -> 0%
where the time goes in v1:
time: 520 us; the launch traced here: 514 us
  waiting for transfers between devices  301 us (58%)
  matrix products  123 us (24%)
  other arithmetic  58.6 us (11%)
  between operations  15.7 us (3%)
  local copies, waits for them, and re-layouts  8.2 us (2%)
  blocking collectives  6.38 us (1%)
    psum x2, waiting for transfers between devices, local(): left = lax.psum(lax.psum(partial_value, 'replica'), 'tensor') / replicas  139 us
    psum x1, waiting for transfers between devices, local(): right = lax.psum(right_part, ('fsdp', 'replica')) / replicas  102 us
    all_gather x1, waiting for transfers between devices, local(): lax.all_gather(basis, 'fsdp', axis=1, tiled=True)  37.4 us
    another operation x6, other arithmetic, local(): chol = jnp.linalg.cholesky(gram)  34 us
    dot_general x1, matrix products, local(): jnp.dot(ortho, right.T, precision=HIGH, preferred_element_type=jnp.float32)  33.1 us
    dot_general x1, matrix products, local(): jnp.dot(buffer.T, ortho, precision=HIGH, preferred_element_type=jnp.float32)  31.3 us
    dot_general x1, matrix products, local(): jnp.dot(ortho, basis_full.T, precision=HIGH, preferred_element_type=jnp.f...  28.8 us
    psum x1, waiting for transfers between devices, local(): gram = lax.psum(local_gram, 'fsdp')  21.2 us
  transfers between devices with their start and end apart: 5, of which 5 were waited for; matrix products, arithmetic and copies ran while one was open for 0% of the time, Pallas kernels for 0%

profile of v1, /device:TPU:0, one launch (start us, length us, event | category | flops | bytes accessed | tf_op | source)
XLA Modules:
  0.0 513.5 jit_solution(10190933296312721603)
XLA Ops:
  7.2 0.0 all-gather.2.cloned.1.call-start
  7.2 0.7 all-gather.2.cloned.1.call-update
  7.9 0.0 all-reduce.6.cloned.1.call-start
  7.9 37.4 %all-gather.2.cloned.1.call-done = f32[2048,256]{1,0:T(8,128)} async-done(((f32[2048,128]{1,0:T(8,128)}), f32[2048,256]{1,0:T(8,128)}) %all-gather.2.cloned.1.call-update) | async-done | bytes 2097168 | tf_op jit(solution)/shard_map/all_gather | solution.py:18
  45.3 18.8 %fusion.2 = f32[2048,256]{1,0:T(8,128)} fusion(f32[2048,256]{1,0:T(8,128)} %all-gather.2.cloned.1.call-done, f32[1,2048,2048]{2,1,0:T(8,128)} %param.4, bf16[1,2048,2048]{2,1,0:T(8,128)(2,1)} %param.3), kind=kOutput, calls=%fused_computation.5 | convolution fusion | flops 12893290496 | bytes 29360128 | tf_op jit(solution)/shard_map/dot_general | solution.py:16
  64.2 0.0 all-reduce.6.cloned.1.call-update
  64.2 0.0 all-reduce.8.cloned.1.call-start
  64.2 86.3 %all-reduce.6.cloned.1.call-done = f32[2048,256]{1,0:T(8,128)} async-done(((f32[2048,256]{1,0:T(8,128)}), f32[2048,256]{1,0:T(8,128)}) %all-reduce.6.cloned.1.call-update) | async-done | bytes 2097168 | tf_op jit(solution)/shard_map/psum | solution.py:22
  150.5 0.0 all-reduce.8.cloned.1.call-update
  150.5 0.0 all-reduce.10.cloned.1.call-start
  150.6 52.7 %all-reduce.8.cloned.1.call-done = f32[2048,256]{1,0:T(8,128)} async-done(((f32[2048,256]{1,0:T(8,128)}), f32[2048,256]{1,0:T(8,128)}) %all-reduce.8.cloned.1.call-update) | async-done | bytes 2097168 | tf_op jit(solution)/shard_map/psum | solution.py:22
  203.3 6.4 %fusion.19 = f32[256,256]{0,1:T(8,128)} fusion(f32[2048,256]{1,0:T(8,128)} %all-reduce.8.cloned.1.call-done), kind=kOutput, calls=%fused_computation.47 | convolution fusion | flops 1611137024 | bytes 2359296 | tf_op jit(solution)/shard_map/dot_general | solution.py:23
  209.7 0.0 all-reduce.10.cloned.1.call-update
  209.7 0.6 all-reduce.12.cloned.1.call-start
  210.3 1.7 broadcast_multiply_fusion
  212.0 21.2 %all-reduce.10.cloned.1.call-done = f32[256,256]{0,1:T(8,128)} async-done(((f32[256,256]{0,1:T(8,128)}), f32[256,256]{0,1:T(8,128)}) %all-reduce.10.cloned.1.call-update) | async-done | bytes 262160 | tf_op jit(solution)/shard_map/psum | solution.py:24
  233.3 1.1 copy.7
  234.4 1.0 fusion.9
  235.4 11.7 %cholesky.50 = f32[128,128]{1,0:T(8,128)S(1)} custom-call(f32[128,128]{1,0:T(8,128)S(1)} %cholesky.118), custom_call_target="Cholesky" | custom-call | tf_op jit(solution)/shard_map/jit(cholesky)/cholesky | solution.py:25
  247.1 9.8 %custom-call.14 = f32[1,128,128]{1,2,0:T(8,128)S(1)} custom-call(f32[1,128,128]{2,1,0:T(8,128)S(1)} %get-tuple-element.24), custom_call_target="InvertDiagBlocksLowerTriangular" | custom-call | tf_op jit(solution)/shard_map/jit(cholesky)/cholesky | solution.py:25
  256.9 0.2 constant_dynamic-update-slice_fusion
  257.2 0.3 convolution_subtract_fusion.1
  257.4 11.7 %cholesky.105 = f32[128,128]{1,0:T(8,128)S(1)} custom-call(f32[128,128]{1,0:T(8,128)S(1)} %convolution_subtract_fusion.1), custom_call_target="Cholesky" | custom-call | tf_op jit(solution)/shard_map/jit(cholesky)/cholesky | solution.py:25
  269.2 0.6 compare_reduce_fusion
  271.2 0.1 triangular_solve.58
  271.2 4.2 while.1
  271.4 0.6 fusion.28
  272.0 1.4 bitcast_dynamic-update-slice_fusion.2
  273.4 0.6 fusion.28
  274.0 1.4 bitcast_dynamic-update-slice_fusion.2
  275.4 19.7 %custom-call.15 = f32[2,128,128]{1,2,0:T(8,128)S(1)} custom-call(f32[2,128,128]{2,1,0:T(8,128)S(1)} %get-tuple-element.10), custom_call_target="InvertDiagBlocksLowerTriangular" | custom-call | tf_op jit(solution)/shard_map/triangular_solve | solution.py:26
  295.1 1.1 fusion.6
  296.2 1.8 convolution_subtract_fusion
  298.0 1.1 fusion.10
  299.1 0.0 copy-start.1
  299.1 1.0 copy-done.1
  300.1 31.3 %fusion = f32[2048,256]{1,0:T(8,128)} fusion(f32[1,2048,2048]{2,1,0:T(8,128)} %param.4, bf16[1,2048,2048]{2,1,0:T(8,128)(2,1)} %param.3, f32[2048,128]{0,1:T(8,128)S(1)} %fusion.10, f32[2048,128]{0,1:T(8,128)S(1)} %fusion.6), kind=kOutput, calls=%fused_computation.3 | convolution fusion | flops 12893814784 | bytes 29360128 | tf_op jit(solution)/shard_map/dot_general | solution.py:27
  331.3 0.0 all-reduce.12.cloned.1.call-update
  331.4 102.4 %all-reduce.12.cloned.1.call-done = f32[2048,256]{1,0:T(8,128)} async-done(((f32[2048,256]{1,0:T(8,128)}), f32[2048,256]{1,0:T(8,128)}) %all-reduce.12.cloned.1.call-update) | async-done | bytes 2097168 | tf_op jit(solution)/shard_map/psum | solution.py:28
  433.8 0.0 copy-start
  433.8 2.0 multiply_reduce_fusion
  435.8 6.4 %psum.39 = f32[256]{0:T(256)S(1)} all-reduce(f32[256]{0:T(256)S(1)} %multiply_reduce_fusion), channel_id=1, replica_groups=mesh['fsdp'=2,'tensor'=4,'replica'=4] {'tensor'}, use_global_device_ids=true, to_apply=%region_9.10 | all-reduce | flops 256 | bytes 2048 | tf_op jit(solution)/shard_map/psum | solution.py:29
  442.2 0.0 copy-done
  442.2 0.1 multiply_divide_fusion
  442.4 1.1 copy-done.2
  443.5 28.8 %multiply_convert_fusion = bf16[2048,2048]{1,0:T(8,128)(2,1)} fusion(f32[2048,256]{1,0:T(8,128)S(1)} %multiply_divide_fusion, f32[2048,128]{0,1:T(8,128)S(1)} %copy-done.2, f32[2048,128]{0,1:T(8,128)S(1)} %fusion.6), kind=kOutput, calls=%fused_computation.8 | convolution fusion | flops 12893814784 | bytes 12582912 | tf_op jit(solution)/shard_map/dot_general | solution.py:36
  472.3 1.0 constant_dynamic-slice_fusion.1
  473.3 33.1 %fusion.4 = f32[1,2048,2048]{2,1,0:T(8,128)} fusion(f32[1,2048,2048]{2,1,0:T(8,128)} %param.4, bf16[1,2048,2048]{2,1,0:T(8,128)(2,1)} %param.3, f32[2048,256]{1,0:T(8,128)S(1)} %copy-done, f32[2048,128]{0,1:T(8,128)S(1)} %copy-done.2, f32[2048,128]{0,1:T(8,128)S(1)} %fusion.6), kind=kOutput, calls=%fused_computation.7 | convolution fusion | flops 12902727680 | bytes 46137344 | tf_op jit(solution)/shard_map/dot_general | solution.py:32
  (11 shorter events, 0.2 us)
Async XLA Ops:
  7.2 38.2 %all-gather.2.cloned.1.call-start = ((), (), s32[]{:S(2)}) async-start(), calls=%async_computation | async-start | bytes 3145728 | tf_op jit(solution)/shard_map/all_gather | solution.py:18
  7.9 142.6 %all-reduce.6.cloned.1.call-start = ((), (), s32[]{:S(2)}) async-start(), calls=%async_computation.1 | async-start | bytes 4194304 | tf_op jit(solution)/shard_map/psum | solution.py:22
  64.2 139.1 %all-reduce.8.cloned.1.call-start = ((), (), s32[]{:S(2)}) async-start(), calls=%async_computation.2 | async-start | bytes 4194304 | tf_op jit(solution)/shard_map/psum | solution.py:22
  150.5 82.7 %all-reduce.10.cloned.1.call-start = ((), (), s32[]{:S(2)}) async-start(), calls=%async_computation.3 | async-start | bytes 524288 | tf_op jit(solution)/shard_map/psum | solution.py:24
  209.7 224.1 %all-reduce.12.cloned.1.call-start = ((), (), s32[]{:S(2)}) async-start(), calls=%async_computation.4 | async-start | bytes 4194304 | tf_op jit(solution)/shard_map/psum | solution.py:28
  299.1 1.0 copy-start.1
  433.8 8.4 %copy-start = (f32[2048,256]{1,0:T(8,128)S(1)}, f32[2048,256]{1,0:T(8,128)}, u32[]{:S(2)}) copy-start(f32[2048,256]{1,0:T(8,128)} %all-reduce.12.cloned.1.call-done) | copy-start | bytes 6291460
  442.2 1.2 copy-start.2
Sparse Core Ops, SparseCore 0:
  9.5 35.7 all-gather.1
  64.3 86.1 all-reduce.5
  152.9 50.3 all-reduce.7
  209.9 23.3 all-reduce.9
  331.5 102.2 all-reduce.11
